TPU v7x, 256 devices: a whole 4x4x8 slice. The times are simulated.
256 devices in a mesh: seq: 32 (over z, y_lo, core), tensor: 8 (over x, y_hi).
Axes of the slice: x: 4, y: 4 (y_hi: 2, y_lo: 2; y = y_hi * 2 + y_lo), z: 8, core: 2. Of those that a mesh axis runs over, the one named last changes fastest.
Arguments:
- hidden_in: bfloat16 [8192, 8192], P('seq', 'tensor'), may hold values from -6 to 6
- frozen_query: bfloat16 [8192, 8192], P('seq', 'tensor'), may hold values from -48 to 48
- key_base: bfloat16 [8192, 1024], P('seq', 'tensor'), may hold values from -6 to 6
- frozen_value: bfloat16 [8192, 1024], P('seq', 'tensor'), may hold values from -6 to 6
- down_query: bfloat16 [8192, 16], P('tensor'), may hold values from -0.0625 to 0.0625
- query_upper_factor: bfloat16 [16, 8192], P(None, 'tensor'), may hold values from -1.5 to 1.5
- down_value: bfloat16 [8192, 16], P('tensor'), may hold values from -0.0625 to 0.0625
- value_upper_factor: bfloat16 [16, 1024], P(None, 'tensor'), may hold values from -1.5 to 1.5
- grad_output: bfloat16 [8192, 8192], P('seq', 'tensor'), may hold values from -6 to 6
Outputs:
- attention: bfloat16 [8192, 8192], P('seq', 'tensor')
- grad_down_query: float32 [8192, 16], P('tensor')
- gradient_query_upper: float32 [16, 8192], P(None, 'tensor')
- grad_down_value: float32 [8192, 16], P('tensor')
- gradient_value_upper: float32 [16, 1024], P(None, 'tensor')
All inputs are finite; a program needn't handle non-finite values.
Results may differ from a plain program's by a relative error of at most 0.024.
Values may be sent and summed in bfloat16 or wider, within the bound.
A program may use at most 128 MiB of HBM per device.

v0:
```python
import jax
import jax.numpy as jnp
from jax import lax
from jax.sharding import PartitionSpec as P

HD = 128
GROUP = 2048


ADAPTER_SCALE = 0.5


def passed_along(block, axis, distance):
    devices = range(lax.axis_size(axis))
    route = [((i - distance) % len(devices), i) for i in devices]
    return lax.ppermute(block, axis, route)


def per_device(
    hidden_in,
    frozen_query,
    key_base,
    frozen_value,
    down_query,
    query_upper_factor,
    down_value,
    value_upper_factor,
    grad_output,
):
    rows_here = hidden_in.shape[0]
    seq_count = lax.axis_size("seq")
    heads_here = frozen_query.shape[1] // HD
    kv_here = key_base.shape[1] // HD
    per_head = heads_here // kv_here
    width_q = heads_here * HD
    width_kv = kv_here * HD
    scale_inv = float(HD) ** (-0.5)
    group_blocks = GROUP // rows_here
    half_blocks = group_blocks // 2
    part_q = jnp.dot(hidden_in, down_query, preferred_element_type=jnp.float32)
    part_v = jnp.dot(hidden_in, down_value, preferred_element_type=jnp.float32)
    sum_q, sum_v = lax.psum((part_q, part_v), "tensor")
    reduced_query = sum_q.astype(jnp.bfloat16)
    reduced_value = sum_v.astype(jnp.bfloat16)
    query_matrix = (
        frozen_query.astype(jnp.float32)
        + ADAPTER_SCALE
        * jnp.dot(reduced_query, query_upper_factor, preferred_element_type=jnp.float32)
    ).astype(jnp.bfloat16)
    value_rows = (
        frozen_value.astype(jnp.float32)
        + ADAPTER_SCALE
        * jnp.dot(reduced_value, value_upper_factor, preferred_element_type=jnp.float32)
    ).astype(jnp.bfloat16)
    shifted = lax.axis_index("tensor") >= lax.axis_size("tensor") // 2
    packed = jnp.concatenate((query_matrix, key_base, value_rows, grad_output), axis=1)
    arrived = passed_along(packed, "seq", seq_count - half_blocks - 1)
    packed = jnp.where(shifted, arrived, packed)
    query_matrix = packed[:, :width_q]
    key_rows = packed[:, width_q : width_q + width_kv]
    value_rows = packed[:, width_q + width_kv : width_q + 2 * width_kv]
    upstream = packed[:, width_q + 2 * width_kv :]
    offset_blocks = jnp.where(shifted, -1, 0).astype(jnp.int32)
    frame_block = (lax.axis_index("seq") - offset_blocks) % seq_count
    place_in_group = frame_block % group_blocks
    own_pair = jnp.concatenate((key_rows, value_rows), axis=1)
    pair_blocks = [own_pair]
    for distance in range(1, group_blocks):
        pair_blocks.append(passed_along(own_pair, "seq", distance))
    query_rows = query_matrix.reshape(rows_here, kv_here, per_head, HD)
    upstream_rows = upstream.reshape(rows_here, kv_here, per_head, HD)
    causal = jnp.arange(rows_here)[:, None] >= jnp.arange(rows_here)[None, :]
    key_list = []
    value_list = []
    kept_scores = []
    for distance in range(group_blocks):
        piece = pair_blocks[distance]
        block_keys = piece[:, :width_kv].reshape(rows_here, kv_here, HD)
        block_values = piece[:, width_kv:].reshape(rows_here, kv_here, HD)
        key_list.append(block_keys)
        value_list.append(block_values)
        scores = (
            jnp.einsum("tgpd,sgd->gpts", query_rows, block_keys, preferred_element_type=jnp.float32)
            * scale_inv
        )
        allow = causal if distance == 0 else place_in_group >= distance
        kept_scores.append(jnp.where(allow, scores, -jnp.inf))
    row_max = jnp.max(kept_scores[0], axis=-1, keepdims=True)
    for distance in range(1, group_blocks):
        row_max = jnp.maximum(row_max, jnp.max(kept_scores[distance], axis=-1, keepdims=True))
    row_total = jnp.sum(jnp.exp(kept_scores[0] - row_max), axis=-1, keepdims=True)
    for distance in range(1, group_blocks):
        row_total = row_total + jnp.sum(
            jnp.exp(kept_scores[distance] - row_max), axis=-1, keepdims=True
        )
    lse = row_max + jnp.log(row_total)
    prob_list = []
    prob_bf_list = []
    out_sum = jnp.zeros((rows_here, kv_here, per_head, HD), jnp.float32)
    for distance in range(group_blocks):
        probs = jnp.exp(kept_scores[distance] - lse)
        kept_scores[distance] = None
        probs_bf = probs.astype(jnp.bfloat16)
        prob_list.append(probs)
        prob_bf_list.append(probs_bf)
        out_sum = out_sum + jnp.einsum(
            "gpts,sgd->tgpd", probs_bf, value_list[distance], preferred_element_type=jnp.float32
        )
    output_bf = out_sum.astype(jnp.bfloat16)
    row_delta = jnp.sum(upstream_rows.astype(jnp.float32) * output_bf.astype(jnp.float32), axis=-1)
    delta_cols = jnp.transpose(row_delta, (1, 2, 0))[..., None]
    grad_query_sum = jnp.zeros((rows_here, kv_here, per_head, HD), jnp.float32)
    value_parts = []
    for distance in range(group_blocks):
        grad_probs = jnp.einsum(
            "tgpd,sgd->gpts",
            upstream_rows,
            value_list[distance],
            preferred_element_type=jnp.float32,
        )
        grad_scores = (prob_list[distance] * (grad_probs - delta_cols) * scale_inv).astype(
            jnp.bfloat16
        )
        grad_query_sum = grad_query_sum + jnp.einsum(
            "gpts,sgd->tgpd", grad_scores, key_list[distance], preferred_element_type=jnp.float32
        )
        value_parts.append(
            jnp.einsum(
                "gpts,tgpd->sgd",
                prob_bf_list[distance],
                upstream_rows,
                preferred_element_type=jnp.float32,
            )
        )
    grad_value_sum = value_parts[0]
    for distance in range(1, group_blocks):
        grad_value_sum = grad_value_sum + passed_along(
            value_parts[distance], "seq", seq_count - distance
        )
    attention = output_bf.reshape(rows_here, width_q)
    query_gradient_rows = grad_query_sum.reshape(rows_here, width_q).astype(jnp.bfloat16)
    value_gradient_rows = grad_value_sum.reshape(rows_here, width_kv).astype(jnp.bfloat16)
    packed = jnp.concatenate((attention, query_gradient_rows, value_gradient_rows), axis=1)
    arrived = passed_along(packed, "seq", half_blocks + 1)
    packed = jnp.where(shifted, arrived, packed)
    attention = packed[:, :width_q]
    query_gradient_rows = packed[:, width_q : 2 * width_q]
    value_gradient_rows = packed[:, 2 * width_q :]
    head_q = jnp.dot(query_gradient_rows, query_upper_factor.T, preferred_element_type=jnp.float32)
    head_v = jnp.dot(value_gradient_rows, value_upper_factor.T, preferred_element_type=jnp.float32)
    returned_query_rows, returned_value_rows = lax.psum((head_q, head_v), "tensor")
    restored_query = (ADAPTER_SCALE * returned_query_rows).astype(jnp.bfloat16)
    restored_value = (ADAPTER_SCALE * returned_value_rows).astype(jnp.bfloat16)
    resident_query_upper = (
        jnp.dot(reduced_query.T, query_gradient_rows, preferred_element_type=jnp.float32)
        * ADAPTER_SCALE
    )
    resident_value_upper = (
        jnp.dot(reduced_value.T, value_gradient_rows, preferred_element_type=jnp.float32)
        * ADAPTER_SCALE
    )
    local_down_q = jnp.dot(hidden_in.T, restored_query, preferred_element_type=jnp.float32)
    local_down_v = jnp.dot(hidden_in.T, restored_value, preferred_element_type=jnp.float32)
    gradient_query_upper, gradient_value_upper, grad_down_query, grad_down_value = (
        lax.psum(resident_query_upper.astype(jnp.bfloat16), "seq").astype(jnp.float32),
        lax.psum(resident_value_upper.astype(jnp.bfloat16), "seq").astype(jnp.float32),
        lax.psum(local_down_q.astype(jnp.bfloat16), "seq").astype(jnp.float32),
        lax.psum(local_down_v.astype(jnp.bfloat16), "seq").astype(jnp.float32),
    )
    return (attention, grad_down_query, gradient_query_upper, grad_down_value, gradient_value_upper)


def solution(mesh):
    placed = (
        P("seq", "tensor"),
        P("seq", "tensor"),
        P("seq", "tensor"),
        P("seq", "tensor"),
        P("tensor", None),
        P(None, "tensor"),
        P("tensor", None),
        P(None, "tensor"),
        P("seq", "tensor"),
    )
    return jax.shard_map(
        per_device,
        mesh=mesh,
        in_specs=placed,
        out_specs=(
            P("seq", "tensor"),
            P("tensor", None),
            P(None, "tensor"),
            P("tensor", None),
            P(None, "tensor"),
        ),
        check_vma=False,
    )
```

profile of v0, /device:TPU:1, one launch (start us, length us, event | category | flops | bytes accessed | tf_op | source)
XLA Modules:
  0.0 520.1 jit_solution(4279358275864707125)
XLA Ops:
  10.2 35.7 %all-reduce.1 = (bf16[256,16]{0,1:T(8,128)(2,1)S(1)}, bf16[256,16]{0,1:T(8,128)(2,1)S(1)}) all-reduce(f32[256,16]{0,1:T(8,128)S(1)} %fusion.207, f32[256,16]{0,1:T(8,128)S(1)} %fusion.206), channel_id=1, replica_groups=mesh['seq'=32,'tensor'=8] {'tensor'}, use_global_device_ids=true, to_apply=%region_1.0 | all-reduce | flops 8192 | bytes 49152 | tf_op jit(solution)/shard_map/psum | solution.py:42
  48.5 13.3 %collective-permute-start = (bf16[256,2304]{1,0:T(8,128)(2,1)S(1)}, bf16[256,2304]{1,0:T(8,128)(2,1)}, u32[]{:S(2)}, u32[]{:S(2)}) collective-permute-start(bf16[256,2304]{1,0:T(8,128)(2,1)S(1)} %pad_maximum_fusion), channel_id=1, source_target_pairs={{40,0},{48,8},{56,16},{64,24},{72,32},{80,40},{88,48},{96,56},{104... | collective-permute-start | bytes 3538952 | tf_op jit(solution)/shard_map/ppermute | solution.py:16
  61.8 32.7 %collective-permute-done = bf16[256,2304]{1,0:T(8,128)(2,1)} collective-permute-done((bf16[256,2304]{1,0:T(8,128)(2,1)S(1)}, bf16[256,2304]{1,0:T(8,128)(2,1)}, u32[]{:S(2)}, u32[]{:S(2)}) %collective-permute-start) | collective-permute-done | bytes 1179680 | tf_op jit(solution)/shard_map/ppermute | solution.py:16
  95.8 3.5 collective-permute-start.7
  100.3 7.2 %collective-permute-start.5 = (bf16[256,256]{1,0:T(8,128)(2,1)}, bf16[256,256]{1,0:T(8,128)(2,1)S(1)}, u32[]{:S(2)}, u32[]{:S(2)}) collective-permute-start(bf16[256,256]{1,0:T(8,128)(2,1)} %concatenate.12), channel_id=1, source_target_pairs={{216,0},{224,8},{232,16},{240,24},{248,32},{0,40},{8,48},{16,56},{... | collective-permute-start | bytes 393224 | tf_op jit(solution)/shard_map/ppermute | solution.py:16
  116.9 5.6 %collective-permute-done.3 = bf16[256,256]{1,0:T(8,128)(2,1)} collective-permute-done((bf16[256,256]{1,0:T(8,128)(2,1)}, bf16[256,256]{1,0:T(8,128)(2,1)}, u32[]{:S(2)}, u32[]{:S(2)}) %collective-permute-start.3) | collective-permute-done | bytes 131104 | tf_op jit(solution)/shard_map/ppermute | solution.py:16
  126.2 4.7 fusion.43
  131.0 3.9 fusion.106
  134.9 2.6 copy.131
  139.7 4.1 collective-permute-start.14
  148.7 4.2 collective-permute-start.13
  157.7 2.6 copy.125
  185.2 3.4 fusion.77
  188.6 3.4 fusion.78
  192.0 3.4 fusion.79
  195.4 3.5 fusion.80
  198.9 3.6 fusion.81
  202.5 3.4 fusion.82
  206.0 3.5 fusion.83
  212.6 5.6 %fusion.75 = bf16[128,8,256]{2,0,1:T(8,128)(2,1)} fusion(f32[128,8,256]{2,0,1:T(8,128)} %fusion.77, f32[128,8,256]{2,0,1:T(8,128)} %fusion.78, f32[128,8,256]{2,0,1:T(8,128)} %fusion.79, f32[128,8,256]{2,0,1:T(8,128)} %fusion.80, f32[128,8,256]{2,0,1:T(8,128)} %fusion.81, f32[128,8,256]{2,0,1:T(8,128)} %fusion.82, f32[128,8,256]{2,0,1:T(8,128)} %fusion.83, ...), kind=kOutput, calls=%fused_computation.117 | convolution fusion | flops 273154048 | bytes 10633216 | tf_op jit(solution)/shard_map/gpts,sgd->tgpd/dot_general | solution.py:124
  222.6 3.2 collective-permute-start.15
  225.9 24.3 %collective-permute-done.15 = bf16[256,2176]{1,0:T(8,128)(2,1)S(1)} collective-permute-done((bf16[256,2176]{1,0:T(8,128)(2,1)S(1)}, bf16[256,2176]{1,0:T(8,128)(2,1)S(1)}, u32[]{:S(2)}, u32[]{:S(2)}) %collective-permute-start.15) | collective-permute-done | bytes 1114144 | tf_op jit(solution)/shard_map/ppermute | solution.py:16
  253.5 33.2 %all-reduce = (f32[256,16]{1,0:T(8,128)S(1)}, f32[256,16]{1,0:T(8,128)S(1)}) all-reduce(f32[256,16]{1,0:T(8,128)S(1)} %fusion.153, f32[256,16]{1,0:T(8,128)S(1)} %fusion.182), channel_id=1, replica_groups=mesh['seq'=32,'tensor'=8] {'tensor'}, use_global_device_ids=true, to_apply=%region_19.20 | all-reduce | flops 8192 | bytes 65536 | tf_op jit(solution)/shard_map/psum | solution.py:151
  289.3 218.0 %all-reduce.5.cloned.1.call-done = (bf16[1024,16]{0,1:T(8,128)(2,1)}, bf16[16,1024]{1,0:T(8,128)(2,1)}, bf16[1024,16]{0,1:T(8,128)(2,1)}, bf16[16,128]{1,0:T(8,128)(2,1)}) async-done(((bf16[1024,16]{0,1:T(8,128)(2,1)}, bf16[16,1024]{1,0:T(8,128)(2,1)}, bf16[1024,16]{0,1:T(8,128)(2,1)}, bf16[16,128]{1,0:T(8,128)(2,1)}), (bf16[1024,16]{0,1:T(8,128)(2,1)}, bf16[16,1024]{1,0:T(8,128)(2,1)}, ...) | async-done | bytes 102416 | tf_op jit(solution)/shard_map/psum | solution.py:167
  (149 shorter events, 76.3 us)
Async XLA Ops:
  7.2 41.2 %copy-start.18 = (bf16[256,1024]{1,0:T(8,128)(2,1)S(1)}, bf16[256,1024]{1,0:T(8,128)(2,1)}, u32[]{:S(2)}) copy-start(bf16[256,1024]{1,0:T(8,128)(2,1)} %param.17) | copy-start | bytes 1572868
  7.2 41.2 %copy-start.24 = (bf16[256,128]{1,0:T(8,128)(2,1)S(1)}, bf16[256,128]{1,0:T(8,128)(2,1)}, u32[]{:S(2)}) copy-start(bf16[256,128]{1,0:T(8,128)(2,1)} %param.11) | copy-start | bytes 196612
  7.2 500.1 %all-reduce.5.cloned.1.call-start = ((), (), s32[]{:S(2)}) async-start(), calls=%async_computation | async-start | bytes 204800 | tf_op jit(solution)/shard_map/psum | solution.py:167
  48.5 46.0 %collective-permute-start = (bf16[256,2304]{1,0:T(8,128)(2,1)S(1)}, bf16[256,2304]{1,0:T(8,128)(2,1)}, u32[]{:S(2)}, u32[]{:S(2)}) collective-permute-start(bf16[256,2304]{1,0:T(8,128)(2,1)S(1)} %pad_maximum_fusion), channel_id=1, source_target_pairs={{40,0},{48,8},{56,16},{64,24},{72,32},{80,40},{88,48},{96,56},{104... | collective-permute-start | bytes 3538952 | tf_op jit(solution)/shard_map/ppermute | solution.py:16
  95.8 14.9 %collective-permute-start.7 = (bf16[256,256]{1,0:T(8,128)(2,1)}, bf16[256,256]{1,0:T(8,128)(2,1)S(1)}, u32[]{:S(2)}, u32[]{:S(2)}) collective-permute-start(bf16[256,256]{1,0:T(8,128)(2,1)} %concatenate.12), channel_id=1, source_target_pairs={{200,0},{208,8},{216,16},{224,24},{232,32},{240,40},{248,48},{0,56... | collective-permute-start | bytes 393224 | tf_op jit(solution)/shard_map/ppermute | solution.py:16
  99.3 12.2 %collective-permute-start.6 = (bf16[256,256]{1,0:T(8,128)(2,1)}, bf16[256,256]{1,0:T(8,128)(2,1)S(1)}, u32[]{:S(2)}, u32[]{:S(2)}) collective-permute-start(bf16[256,256]{1,0:T(8,128)(2,1)} %concatenate.12), channel_id=1, source_target_pairs={{208,0},{216,8},{224,16},{232,24},{240,32},{248,40},{0,48},{8,56},... | collective-permute-start | bytes 393224 | tf_op jit(solution)/shard_map/ppermute | solution.py:16
  100.3 13.5 %collective-permute-start.5 = (bf16[256,256]{1,0:T(8,128)(2,1)}, bf16[256,256]{1,0:T(8,128)(2,1)S(1)}, u32[]{:S(2)}, u32[]{:S(2)}) collective-permute-start(bf16[256,256]{1,0:T(8,128)(2,1)} %concatenate.12), channel_id=1, source_target_pairs={{216,0},{224,8},{232,16},{240,24},{248,32},{0,40},{8,48},{16,56},{... | collective-permute-start | bytes 393224 | tf_op jit(solution)/shard_map/ppermute | solution.py:16
  107.5 8.1 %collective-permute-start.4 = (bf16[256,256]{1,0:T(8,128)(2,1)}, bf16[256,256]{1,0:T(8,128)(2,1)}, u32[]{:S(2)}, u32[]{:S(2)}) collective-permute-start(bf16[256,256]{1,0:T(8,128)(2,1)} %concatenate.12), channel_id=1, source_target_pairs={{224,0},{232,8},{240,16},{248,24},{0,32},{8,40},{16,48},{24,56},{3... | collective-permute-start | bytes 393224 | tf_op jit(solution)/shard_map/ppermute | solution.py:16
  107.5 15.0 %collective-permute-start.3 = (bf16[256,256]{1,0:T(8,128)(2,1)}, bf16[256,256]{1,0:T(8,128)(2,1)}, u32[]{:S(2)}, u32[]{:S(2)}) collective-permute-start(bf16[256,256]{1,0:T(8,128)(2,1)} %concatenate.12), channel_id=1, source_target_pairs={{232,0},{240,8},{248,16},{0,24},{8,32},{16,40},{24,48},{32,56},{40... | collective-permute-start | bytes 393224 | tf_op jit(solution)/shard_map/ppermute | solution.py:16
  110.8 14.2 %collective-permute-start.2 = (bf16[256,256]{1,0:T(8,128)(2,1)}, bf16[256,256]{1,0:T(8,128)(2,1)S(1)}, u32[]{:S(2)}, u32[]{:S(2)}) collective-permute-start(bf16[256,256]{1,0:T(8,128)(2,1)} %concatenate.12), channel_id=1, source_target_pairs={{240,0},{248,8},{0,16},{8,24},{16,32},{24,40},{32,48},{40,56},{48,... | collective-permute-start | bytes 393224 | tf_op jit(solution)/shard_map/ppermute | solution.py:16
  111.5 13.9 %collective-permute-start.1 = (bf16[256,256]{1,0:T(8,128)(2,1)}, bf16[256,256]{1,0:T(8,128)(2,1)S(1)}, u32[]{:S(2)}, u32[]{:S(2)}) collective-permute-start(bf16[256,256]{1,0:T(8,128)(2,1)} %concatenate.12), channel_id=1, source_target_pairs={{248,0},{0,8},{8,16},{16,24},{24,32},{32,40},{40,48},{48,56},{56,6... | collective-permute-start | bytes 393224 | tf_op jit(solution)/shard_map/ppermute | solution.py:16
  125.0 57.8 %copy-start.20 = (bf16[256,256]{1,0:T(8,128)(2,1)}, bf16[256,256]{1,0:T(8,128)(2,1)S(1)}, u32[]{:S(2)}) copy-start(bf16[256,256]{1,0:T(8,128)(2,1)S(1)} %collective-permute-done.2) | copy-start | bytes 393220
  125.4 57.7 %copy-start.22 = (bf16[256,256]{1,0:T(8,128)(2,1)}, bf16[256,256]{1,0:T(8,128)(2,1)S(1)}, u32[]{:S(2)}) copy-start(bf16[256,256]{1,0:T(8,128)(2,1)S(1)} %collective-permute-done.1) | copy-start | bytes 393220
  139.7 71.9 %collective-permute-start.14 = (f32[256,1,128]{0,2,1:T(8,128)}, f32[256,1,128]{0,2,1:T(8,128)}, u32[]{:S(2)}, u32[]{:S(2)}) collective-permute-start(f32[256,1,128]{0,2,1:T(8,128)} %convolution_bitcast_fusion), channel_id=1, source_target_pairs={{56,0},{64,8},{72,16},{80,24},{88,32},{96,40},{104,48},{112,56},{1... | collective-permute-start | bytes 393224 | tf_op jit(solution)/shard_map/ppermute | solution.py:16
  148.7 63.7 %collective-permute-start.13 = (f32[256,1,128]{0,2,1:T(8,128)}, f32[256,1,128]{0,2,1:T(8,128)}, u32[]{:S(2)}, u32[]{:S(2)}) collective-permute-start(f32[256,1,128]{0,2,1:T(8,128)} %convolution_bitcast_fusion.1), channel_id=1, source_target_pairs={{48,0},{56,8},{64,16},{72,24},{80,32},{88,40},{96,48},{104,56},{11... | collective-permute-start | bytes 393224 | tf_op jit(solution)/shard_map/ppermute | solution.py:16
  157.7 62.7 %collective-permute-start.12 = (f32[256,1,128]{0,2,1:T(8,128)}, f32[256,1,128]{0,2,1:T(8,128)}, u32[]{:S(2)}, u32[]{:S(2)}) collective-permute-start(f32[256,1,128]{0,2,1:T(8,128)} %convolution_bitcast_fusion.2), channel_id=1, source_target_pairs={{40,0},{48,8},{56,16},{64,24},{72,32},{80,40},{88,48},{96,56},{104... | collective-permute-start | bytes 393224 | tf_op jit(solution)/shard_map/ppermute | solution.py:16
  162.6 57.8 %collective-permute-start.11 = (f32[256,1,128]{0,2,1:T(8,128)}, f32[256,1,128]{0,2,1:T(8,128)}, u32[]{:S(2)}, u32[]{:S(2)}) collective-permute-start(f32[256,1,128]{0,2,1:T(8,128)} %convolution_bitcast_fusion.3), channel_id=1, source_target_pairs={{32,0},{40,8},{48,16},{56,24},{64,32},{72,40},{80,48},{88,56},{96,... | collective-permute-start | bytes 393224 | tf_op jit(solution)/shard_map/ppermute | solution.py:16
  168.9 51.5 %collective-permute-start.10 = (f32[256,1,128]{0,2,1:T(8,128)}, f32[256,1,128]{0,2,1:T(8,128)}, u32[]{:S(2)}, u32[]{:S(2)}) collective-permute-start(f32[256,1,128]{0,2,1:T(8,128)} %convolution_bitcast_fusion.4), channel_id=1, source_target_pairs={{24,0},{32,8},{40,16},{48,24},{56,32},{64,40},{72,48},{80,56},{88,... | collective-permute-start | bytes 393224 | tf_op jit(solution)/shard_map/ppermute | solution.py:16
  211.7 8.8 %collective-permute-start.9 = (f32[256,1,128]{0,2,1:T(8,128)S(1)}, f32[256,1,128]{0,2,1:T(8,128)S(1)}, u32[]{:S(2)}, u32[]{:S(2)}) collective-permute-start(f32[256,1,128]{0,2,1:T(8,128)S(1)} %copy-done.25), channel_id=1, source_target_pairs={{16,0},{24,8},{32,16},{40,24},{48,32},{56,40},{64,48},{72,56},{80,... | collective-permute-start | bytes 393224 | tf_op jit(solution)/shard_map/ppermute | solution.py:16
  212.3 8.1 %collective-permute-start.8 = (f32[256,1,128]{0,2,1:T(8,128)}, f32[256,1,128]{0,2,1:T(8,128)S(1)}, u32[]{:S(2)}, u32[]{:S(2)}) collective-permute-start(f32[256,1,128]{0,2,1:T(8,128)} %convolution_bitcast_fusion.6), channel_id=1, source_target_pairs={{8,0},{16,8},{24,16},{32,24},{40,32},{48,40},{56,48},{64,56},{72,6... | collective-permute-start | bytes 393224 | tf_op jit(solution)/shard_map/ppermute | solution.py:16
  222.6 29.3 %copy-start.31 = (bf16[16,128]{1,0:T(8,128)(2,1)S(1)}, bf16[16,128]{1,0:T(8,128)(2,1)}, u32[]{:S(2)}) copy-start(bf16[16,128]{1,0:T(8,128)(2,1)} %param.16) | copy-start | bytes 12292
  222.6 29.4 %copy-start.27 = (bf16[256,16]{0,1:T(8,128)(2,1)S(1)}, bf16[256,16]{0,1:T(8,128)(2,1)}, u32[]{:S(2)}) copy-start(bf16[256,16]{0,1:T(8,128)(2,1)} %copy-done.26) | copy-start | bytes 24580
  222.6 30.2 %copy-start.30 = (bf16[256,16]{0,1:T(8,128)(2,1)S(1)}, bf16[256,16]{0,1:T(8,128)(2,1)}, u32[]{:S(2)}) copy-start(bf16[256,16]{0,1:T(8,128)(2,1)} %copy-done.29) | copy-start | bytes 24580
  222.6 27.6 %collective-permute-start.15 = (bf16[256,2176]{1,0:T(8,128)(2,1)S(1)}, bf16[256,2176]{1,0:T(8,128)(2,1)S(1)}, u32[]{:S(2)}, u32[]{:S(2)}) collective-permute-start(bf16[256,2176]{1,0:T(8,128)(2,1)S(1)} %pad_maximum_fusion.1), channel_id=1, source_target_pairs={{216,0},{224,8},{232,16},{240,24},{248,32},{0,40},{8,48},{16,56},{... | collective-permute-start | bytes 3342344 | tf_op jit(solution)/shard_map/ppermute | solution.py:16
  (25 other events, 163.8 us)
Sparse Core Ops, SparseCore 0:
  288.6 218.7 all-reduce.4
where the time goes:
time: 528 us; the launch traced here: 520 us
  waiting for transfers between devices  283 us (54%)
  matrix products  69 us (13%)
  blocking collectives  68.9 us (13%)
  starting transfers between devices  41.8 us (8%)
  local copies, waits for them, and re-layouts  25.8 us (5%)
  other arithmetic  16.3 us (3%)
  between operations  15.1 us (3%)
    psum x1, waiting for transfers between devices, per_device(): lax.psum(local_down_q.astype(jnp.bfloat16), 'seq').astype(jnp.float32)  218 us
    ppermute x16, waiting for transfers between devices, passed_along(): return lax.ppermute(block, axis, route)  65.1 us
    ppermute x16, starting transfers between devices, passed_along(): return lax.ppermute(block, axis, route)  41.7 us
    psum x1, blocking collectives, per_device(): sum_q, sum_v = lax.psum((part_q, part_v), 'tensor')  35.7 us
    psum x1, blocking collectives, per_device(): lax.psum((head_q, head_v), 'tensor')  33.2 us
    dot_general x8, matrix products, per_device(): jnp.einsum('gpts,sgd->tgpd', grad_scores, key_list[distance], preferred_e...  29.8 us
    another operation x8, local copies, waits for them, and re-layouts  20.3 us
    dot_general x8, matrix products, per_device(): jnp.einsum('gpts,tgpd->sgd', prob_bf_list[distance], upstream_rows, prefe...  17.5 us
  transfers between devices with their start and end apart: 17, of which 6 were waited for; matrix products, arithmetic and copies ran while one was open for 15% of the time, Pallas kernels for 0%

commit v1 on v0

v1 whole, which is shorter than its diff:
```python
import jax
import jax.numpy as jnp
from jax import lax
from jax.experimental import pallas as pl
from jax.experimental.pallas import tpu as pltpu
from jax.sharding import PartitionSpec as P

HD = 128
GROUP = 2048
ADAPTER_SCALE = 0.5
MESH = pl.DeviceIdType.MESH
F32 = jnp.float32
BF16 = jnp.bfloat16
NT = (((1,), (1,)), ((), ()))
TN = (((0,), (0,)), ((), ()))


def mm(a, b, dims=(((1,), (0,)), ((), ()))):
    return lax.dot_general(a, b, dims, preferred_element_type=F32)


class Spot:
    def __init__(self, seq_count, tensor_count, members):
        self.seq_count, self.tensor_count, self.members = seq_count, tensor_count, members
        self.seq = lax.axis_index("seq")
        self.tensor = lax.axis_index("tensor")
        self.shift = jnp.where(self.tensor >= tensor_count // 2, members // 2, 0).astype(jnp.int32)
        frame = lax.rem(self.seq - self.shift + seq_count, seq_count)
        self.place = lax.rem(frame, members)
        self.base = frame - self.place + self.shift

    def member(self, place):
        return {"seq": lax.rem(self.base + place, self.seq_count), "tensor": self.tensor}

    def across(self, distance):
        return {"seq": self.seq, "tensor": lax.rem(self.tensor + distance, self.tensor_count)}

    def along(self, distance):
        return {"seq": lax.rem(self.seq + distance, self.seq_count), "tensor": self.tensor}


def remote(src, dst, send, recv, device):
    return pltpu.make_async_remote_copy(
        src_ref=src, dst_ref=dst, send_sem=send, recv_sem=recv, device_id=device, device_id_type=MESH
    )


def gather_kernel(
    sizes,
    hidden, down_q, down_v, keys, frozen_v,
    low_out, keys_out, values_out, lowv_out,
    part_slots, low_buf,
    part_send, part_recv, kv_send, kv_recv, low_send, low_recv, local_sem,
):
    spot = Spot(*sizes)
    members, count = spot.members, spot.tensor_count
    place, me = spot.place, spot.tensor
    barrier = pltpu.get_barrier_semaphore()
    for distance in range(1, count):
        pl.semaphore_signal(barrier, inc=1, device_id=spot.across(distance), device_id_type=MESH)
    for distance in range(1, members):
        pl.semaphore_signal(
            barrier, inc=1, device_id=spot.member(lax.rem(place + distance, members)), device_id_type=MESH
        )
    h = hidden[...]
    part_slots[me, 0:16, :] = mm(down_q[...], h, NT).astype(BF16)
    part_slots[me, 16:32, :] = mm(down_v[...], h, NT).astype(BF16)
    pl.semaphore_wait(barrier, count + members - 2)

    def part_copy(distance):
        return remote(
            part_slots.at[me], part_slots.at[me], part_send.at[distance], part_recv.at[me], spot.across(distance)
        )

    for distance in range(1, count):
        part_copy(distance).start()

    def kv_copies(distance):
        peer = spot.member(place + distance)
        return (
            remote(keys, keys_out.at[place], kv_send.at[0, distance], kv_recv.at[0, place], peer),
            remote(frozen_v, values_out.at[place], kv_send.at[1, distance], kv_recv.at[1, place], peer),
        )

    for distance in range(1, members):

        @pl.when(place + distance < members)
        def _():
            for copy in kv_copies(distance):
                copy.start()

    own_copies = (
        pltpu.make_async_copy(keys, keys_out.at[place], local_sem.at[0]),
        pltpu.make_async_copy(frozen_v, values_out.at[place], local_sem.at[1]),
    )
    for copy in own_copies:
        copy.start()
    for distance in range(1, count):
        source = lax.rem(me + distance, count)
        remote(
            part_slots.at[source], part_slots.at[source], part_send.at[0], part_recv.at[source], spot.across(distance)
        ).wait_recv()
    total = part_slots[0].astype(F32)
    for source in range(1, count):
        total = total + part_slots[source].astype(F32)
    low = total.astype(BF16)
    low_out[...] = low
    low_buf[...] = low[16:32]

    def low_copy(distance):
        return remote(
            low_buf, lowv_out.at[place], low_send.at[distance], low_recv.at[place], spot.member(place + distance)
        )

    for distance in range(1, members):

        @pl.when(place + distance < members)
        def _():
            low_copy(distance).start()

    own_low = pltpu.make_async_copy(low_buf, lowv_out.at[place], local_sem.at[2])
    own_low.start()
    for distance in range(1, members):

        @pl.when(place - distance >= 0)
        def _():
            source = place - distance
            peer = spot.member(source)
            remote(keys, keys_out.at[source], kv_send.at[0, 0], kv_recv.at[0, source], peer).wait_recv()
            remote(frozen_v, values_out.at[source], kv_send.at[1, 0], kv_recv.at[1, source], peer).wait_recv()
            remote(low_buf, lowv_out.at[source], low_send.at[0], low_recv.at[source], peer).wait_recv()

    for copy in own_copies:
        copy.wait()
    own_low.wait()
    for distance in range(1, count):
        part_copy(distance).wait_send()
    for distance in range(1, members):

        @pl.when(place + distance < members)
        def _():
            for copy in kv_copies(distance):
                copy.wait_send()
            low_copy(distance).wait_send()


def attention_kernel(
    sizes,
    low, keys, frozen_v, lowv, frozen_q, upper_q, upper_v, upstream,
    att, back_q, back_v, grad_uq, grad_uv,
    q_buf, v_buf, s_buf, p_buf, m_buf, l_buf, o_buf, dq_acc, dq_buf, dv_buf,
):
    spot = Spot(*sizes)
    place = spot.place
    rows = frozen_q.shape[0]
    heads = frozen_q.shape[1] // HD
    scale = float(HD) ** -0.5

    q_buf[...] = (frozen_q[...].astype(F32) + ADAPTER_SCALE * mm(low[0:16, :], upper_q[...], TN)).astype(BF16)

    def value_block(j, carry):
        v_buf[j] = (frozen_v[j].astype(F32) + ADAPTER_SCALE * mm(lowv[j], upper_v[...], TN)).astype(BF16)
        dv_buf[j] = jnp.zeros((HD, rows), F32)
        return carry

    lax.fori_loop(0, place + 1, value_block, 0)

    def span(j):
        return pl.ds(pl.multiple_of(j * rows, rows), rows)

    def wide(x):
        return jnp.concatenate((x,) * (rows // HD), axis=1)

    def halves(f, x):
        out = x[:, :HD]
        for at in range(HD, rows, HD):
            out = f(out, x[:, at : at + HD])
        return out

    def head(h, carry):
        cols = pl.ds(pl.multiple_of(h * HD, HD), HD)
        q = q_buf[:, cols]
        g = upstream[:, cols]
        s = mm(q, keys[place], NT)
        causal = lax.broadcasted_iota(jnp.int32, (rows, rows), 0) >= lax.broadcasted_iota(jnp.int32, (rows, rows), 1)
        s = jnp.where(causal, s, -jnp.inf)
        s_buf[:, span(place)] = s
        m_buf[...] = halves(jnp.maximum, s)

        def score(j, carry):
            s = mm(q, keys[j], NT)
            s_buf[:, span(j)] = s
            m_buf[...] = jnp.maximum(m_buf[...], halves(jnp.maximum, s))
            return carry

        lax.fori_loop(0, place, score, 0)
        m = jnp.broadcast_to(jnp.max(m_buf[...], axis=1, keepdims=True), (rows, HD))
        l_buf[...] = jnp.zeros((rows, HD), F32)
        o_buf[...] = jnp.zeros((rows, HD), F32)

        def weigh(j, carry):
            p = jnp.exp((s_buf[:, span(j)] - wide(m)) * scale)
            s_buf[:, span(j)] = p
            l_buf[...] += halves(jnp.add, p)
            pb = p.astype(BF16)
            p_buf[:, span(j)] = pb
            o_buf[...] += mm(pb, v_buf[j])
            return carry

        lax.fori_loop(0, place + 1, weigh, 0)
        inv = jnp.broadcast_to(1.0 / jnp.sum(l_buf[...], axis=1, keepdims=True), (rows, HD))
        o = (o_buf[...] * inv).astype(BF16)
        att[:, cols] = o
        gf = g.astype(F32)
        delta = jnp.broadcast_to(jnp.sum(gf * o.astype(F32), axis=1, keepdims=True), (rows, HD))
        gt = jnp.transpose((gf * inv).astype(BF16))
        weight = inv * scale
        dq_acc[...] = jnp.zeros((rows, HD), F32)

        def back(j, carry):
            dp = mm(g, v_buf[j], NT)
            ds = (s_buf[:, span(j)] * ((dp - wide(delta)) * wide(weight))).astype(BF16)
            dq_acc[...] += mm(ds, keys[j])
            dv_buf[j] += mm(gt, p_buf[:, span(j)])
            return carry

        lax.fori_loop(0, place + 1, back, 0)
        dq_buf[:, cols] = dq_acc[...].astype(BF16)
        return carry

    lax.fori_loop(0, heads, head, 0)
    dq = dq_buf[...]
    back_q[...] = mm(upper_q[...], dq, NT)
    grad_uq[...] = mm(low[0:16, :], dq) * ADAPTER_SCALE
    grad_uv[...] = jnp.zeros_like(grad_uv)
    back_v[...] = jnp.zeros_like(back_v)

    def value_back(j, carry):
        dv = dv_buf[j].astype(BF16)
        back_v[j] = mm(upper_v[...], dv).astype(BF16)
        grad_uv[...] += mm(lowv[j], dv, NT) * ADAPTER_SCALE
        return carry

    lax.fori_loop(0, place + 1, value_back, 0)


def reduce_kernel(
    sizes,
    hidden, back_q, back_v, grad_uq, grad_uv,
    down_q_out, down_v_out, upper_q_out, upper_v_out,
    group_slots, back_acc, part_slots, stage, sum_slots, result,
    group_send, group_recv, part_send, part_recv, sum_send, sum_recv, out_send, out_recv,
):
    spot = Spot(*sizes)
    members, count, seq_count = spot.members, spot.tensor_count, spot.seq_count
    place, me, seq = spot.place, spot.tensor, spot.seq
    chunks = stage.shape[0]
    barrier = pltpu.get_barrier_semaphore()
    for distance in range(1, count):
        pl.semaphore_signal(barrier, inc=1, device_id=spot.across(distance), device_id_type=MESH)

    def greet(distance, carry):
        pl.semaphore_signal(barrier, inc=1, device_id=spot.along(distance), device_id_type=MESH)
        return carry

    lax.fori_loop(1, seq_count, greet, 0)
    lanes = 128
    for at in range(8):
        stage[16 + at] = grad_uq[:, at * lanes : (at + 1) * lanes].astype(BF16)
    stage[24] = grad_uv[...].astype(BF16)
    pl.semaphore_wait(barrier, count + seq_count - 2)

    def group_copy(distance):
        target = place - distance
        return remote(
            back_v.at[target], group_slots.at[place], group_send.at[distance], group_recv.at[place], spot.member(target)
        )

    for distance in range(1, members):

        @pl.when(place - distance >= 0)
        def _():
            group_copy(distance).start()

    def sum_copy(chunk, distance):
        return remote(
            stage.at[chunk], sum_slots.at[seq], sum_send.at[distance], sum_recv.at[seq], spot.along(distance)
        )

    def send_chunks(first, last):
        def body(distance, carry):
            chunk = lax.rem(seq + distance, seq_count)

            @pl.when((chunk >= first) & (chunk < last))
            def _():
                sum_copy(chunk, distance).start()

            return carry

        lax.fori_loop(1, seq_count, body, 0)

    send_chunks(16, chunks)
    part_slots[me, 0:16, :] = back_q[...].astype(BF16)
    back_acc[...] = back_v[place].astype(F32)
    for distance in range(1, members):

        @pl.when(place + distance < members)
        def _():
            source = place + distance
            remote(
                back_v.at[place], group_slots.at[source], group_send.at[0], group_recv.at[source], spot.member(source)
            ).wait_recv()
            back_acc[...] += group_slots[source].astype(F32)

    part_slots[me, 16:32, :] = back_acc[...].astype(BF16)

    def part_copy(distance):
        return remote(
            part_slots.at[me], part_slots.at[me], part_send.at[distance], part_recv.at[me], spot.across(distance)
        )

    for distance in range(1, count):
        part_copy(distance).start()
    for distance in range(1, count):
        source = lax.rem(me + distance, count)
        remote(
            part_slots.at[source], part_slots.at[source], part_send.at[0], part_recv.at[source], spot.across(distance)
        ).wait_recv()
    total = part_slots[0].astype(F32)
    for source in range(1, count):
        total = total + part_slots[source].astype(F32)
    restored = (ADAPTER_SCALE * total).astype(BF16)
    grad_down = mm(restored, hidden[...])
    for at in range(8):
        stage[at] = grad_down[0:16, at * lanes : (at + 1) * lanes].astype(BF16)
        stage[8 + at] = grad_down[16:32, at * lanes : (at + 1) * lanes].astype(BF16)
    send_chunks(0, 16)

    def out_copy(distance):
        return remote(
            result.at[seq], result.at[seq], out_send.at[distance], out_recv.at[seq], spot.along(distance)
        )

    @pl.when(seq < chunks)
    def _():
        sum_slots[seq] = stage[seq]

        def arrive(distance, carry):
            source = lax.rem(seq + distance, seq_count)
            remote(
                stage.at[0], sum_slots.at[source], sum_send.at[0], sum_recv.at[source], spot.along(distance)
            ).wait_recv()
            return carry

        lax.fori_loop(1, seq_count, arrive, 0)

        def add(source, total):
            return total + sum_slots[source].astype(F32)

        result[seq] = lax.fori_loop(0, seq_count, add, jnp.zeros((16, lanes), F32)).astype(BF16)

        def send(distance, carry):
            out_copy(distance).start()
            return carry

        lax.fori_loop(1, seq_count, send, 0)

    def collect(distance, carry):
        source = lax.rem(seq + distance, seq_count)

        @pl.when(source < chunks)
        def _():
            remote(
                result.at[source], result.at[source], out_send.at[0], out_recv.at[source], spot.along(distance)
            ).wait_recv()

        return carry

    lax.fori_loop(1, seq_count, collect, 0)
    for at in range(8):
        cols = slice(at * lanes, (at + 1) * lanes)
        down_q_out[:, cols] = result[at].astype(F32)
        down_v_out[:, cols] = result[8 + at].astype(F32)
        upper_q_out[:, cols] = result[16 + at].astype(F32)
    upper_v_out[...] = result[24].astype(F32)

    for distance in range(1, members):

        @pl.when(place - distance >= 0)
        def _():
            group_copy(distance).wait_send()

    for distance in range(1, count):
        part_copy(distance).wait_send()

    def drain(distance, carry):
        chunk = lax.rem(seq + distance, seq_count)

        @pl.when(chunk < chunks)
        def _():
            sum_copy(chunk, distance).wait_send()

        @pl.when(seq < chunks)
        def _():
            out_copy(distance).wait_send()

        return carry

    lax.fori_loop(1, seq_count, drain, 0)


def per_device(
    hidden_in,
    frozen_query,
    key_base,
    frozen_value,
    down_query,
    query_upper_factor,
    down_value,
    value_upper_factor,
    grad_output,
):
    rows, width = hidden_in.shape
    rank = down_query.shape[1]
    seq_count, count = lax.axis_size("seq"), lax.axis_size("tensor")
    members = GROUP // rows
    sizes = (seq_count, count, members)
    chunks = 25
    vmem = pl.BlockSpec(memory_space=pltpu.VMEM)
    anywhere = pl.BlockSpec(memory_space=pl.ANY)
    dma = pltpu.SemaphoreType.DMA

    def shape(*dims, dtype=BF16):
        return jax.ShapeDtypeStruct(dims, dtype)

    low, keys, frozen_v, lowv = pl.pallas_call(
        lambda *refs: gather_kernel(sizes, *refs),
        out_shape=(
            shape(2 * rank, rows),
            shape(members, rows, HD),
            shape(members, rows, HD),
            shape(members, rank, rows),
        ),
        in_specs=[vmem] * 5,
        out_specs=(vmem, anywhere, anywhere, anywhere),
        scratch_shapes=[
            pltpu.VMEM((count, 2 * rank, rows), BF16),
            pltpu.VMEM((rank, rows), BF16),
            dma((count,)),
            dma((count,)),
            dma((2, members)),
            dma((2, members)),
            dma((members,)),
            dma((members,)),
            dma((3,)),
        ],
        compiler_params=pltpu.CompilerParams(collective_id=0, has_side_effects=True),
        name="gather",
    )(hidden_in, down_query.T, down_value.T, key_base, frozen_value)

    attention, back_q, back_v, grad_uq, grad_uv = pl.pallas_call(
        lambda *refs: attention_kernel(sizes, *refs),
        out_shape=(
            shape(rows, width),
            shape(rank, rows, dtype=F32),
            shape(members, rank, rows),
            shape(rank, width, dtype=F32),
            shape(rank, HD, dtype=F32),
        ),
        in_specs=[vmem] * 8,
        out_specs=(vmem,) * 5,
        scratch_shapes=[
            pltpu.VMEM((rows, width), BF16),
            pltpu.VMEM((members, rows, HD), BF16),
            pltpu.VMEM((rows, GROUP), F32),
            pltpu.VMEM((rows, GROUP), BF16),
            pltpu.VMEM((rows, HD), F32),
            pltpu.VMEM((rows, HD), F32),
            pltpu.VMEM((rows, HD), F32),
            pltpu.VMEM((rows, HD), F32),
            pltpu.VMEM((rows, width), BF16),
            pltpu.VMEM((members, HD, rows), F32),
        ],
        name="attention",
    )(low, keys, frozen_v, lowv, frozen_query, query_upper_factor, value_upper_factor, grad_output)

    down_q, down_v, upper_q, upper_v = pl.pallas_call(
        lambda *refs: reduce_kernel(sizes, *refs),
        out_shape=(
            shape(rank, width, dtype=F32),
            shape(rank, width, dtype=F32),
            shape(rank, width, dtype=F32),
            shape(rank, HD, dtype=F32),
        ),
        in_specs=[vmem] * 5,
        out_specs=(vmem,) * 4,
        scratch_shapes=[
            pltpu.VMEM((members, rank, rows), BF16),
            pltpu.VMEM((rank, rows), F32),
            pltpu.VMEM((count, 2 * rank, rows), BF16),
            pltpu.VMEM((chunks, rank, 128), BF16),
            pltpu.VMEM((seq_count, rank, 128), BF16),
            pltpu.VMEM((chunks, rank, 128), BF16),
            dma((members,)),
            dma((members,)),
            dma((count,)),
            dma((count,)),
            dma((seq_count,)),
            dma((seq_count,)),
            dma((seq_count,)),
            dma((seq_count,)),
        ],
        compiler_params=pltpu.CompilerParams(collective_id=1, has_side_effects=True),
        name="reduce",
    )(hidden_in, back_q, back_v, grad_uq, grad_uv)
    return (attention, down_q.T, upper_q, down_v.T, upper_v)


def solution(mesh):
    placed = (
        P("seq", "tensor"),
        P("seq", "tensor"),
        P("seq", "tensor"),
        P("seq", "tensor"),
        P("tensor", None),
        P(None, "tensor"),
        P("tensor", None),
        P(None, "tensor"),
        P("seq", "tensor"),
    )
    return jax.shard_map(
        per_device,
        mesh=mesh,
        in_specs=placed,
        out_specs=(
            P("seq", "tensor"),
            P("tensor", None),
            P(None, "tensor"),
            P("tensor", None),
            P(None, "tensor"),
        ),
        check_vma=False,
    )
```

time: 528 us -> 117 us (0.22); the launches traced: 520 us -> 117 us
  waiting for transfers between devices: 283 us -> 0 us
  Pallas kernels: 0 us -> 113 us
  matrix products: 69 us -> 0 us
  blocking collectives: 68.9 us -> 0 us
  starting transfers between devices: 41.8 us -> 0 us
  local copies, waits for them, and re-layouts: 25.8 us -> 3.67 us
  other arithmetic: 16.3 us -> 0 us
  between operations: 15.1 us -> 0.66 us
    psum x1 -> x0, waiting for transfers between devices: 218 us -> none  [per_device(): lax.psum(local_down_q.astype(jnp.bfloat16), 'seq').astype(jnp.float32)]
    pallas_call x0 -> x3, Pallas kernels: none -> 113 us  [the longest x1 73.8 us: per_device(): pl.pallas_call(lambda *refs: reduce_kernel(sizes, *refs), out_shape=(shap...]
    dot_general x42 -> x0, matrix products: 69 us -> none  [the longest x8 29.8 us: per_device(): jnp.einsum('gpts,sgd->tgpd', grad_scores, key_list[distance], preferred_e...]
    psum x2 -> x0, blocking collectives: 68.9 us -> none  [the longest x1 35.7 us: per_device(): sum_q, sum_v = lax.psum((part_q, part_v), 'tensor')]
    ppermute x16 -> x0, waiting for transfers between devices: 65.1 us -> none  [passed_along(): return lax.ppermute(block, axis, route)]
    ppermute x16 -> x0, starting transfers between devices: 41.7 us -> none  [passed_along(): return lax.ppermute(block, axis, route)]
    another operation x8 -> x0, local copies, waits for them, and re-layouts: 20.3 us -> none
    convert_element_type x4 -> x0, other arithmetic: 5.45 us -> none  [the longest x1 1.39 us: per_device(): lax.psum(local_down_q.astype(jnp.bfloat16), 'seq').astype(jnp.float32)]
  transfers between devices with their start and end apart: 17 -> 0, of which waited for: 6 -> 0; matrix products, arithmetic and copies ran while one was open for 15% -> 0% of each run, Pallas kernels for 0% -> 0%
where the time goes in v1:
time: 117 us
  Pallas kernels  113 us (97%)
  local copies, waits for them, and re-layouts  3.67 us (3%)
    pallas_call x1, Pallas kernels, per_device(): pl.pallas_call(lambda *refs: reduce_kernel(sizes, *refs), out_shape=(shap...  73.8 us
    pallas_call x1, Pallas kernels, per_device(): pl.pallas_call(lambda *refs: gather_kernel(sizes, *refs), out_shape=(shap...  20 us
    pallas_call x1, Pallas kernels, per_device(): pl.pallas_call(lambda *refs: attention_kernel(sizes, *refs), out_shape=(s...  18.8 us
    unnamed x10, local copies, waits for them, and re-layouts  3.67 us

profile of v1, /device:TPU:1, one launch (start us, length us, event | category | flops | bytes accessed | tf_op | source)
XLA Modules:
  0.0 117.0 jit_solution(7980720561072032776)
XLA Ops:
  0.6 20.0 %gather.1 = (bf16[32,256]{1,0:T(8,128)(2,1)}, bf16[8,256,128]{2,1,0:T(8,128)(2,1)}, bf16[8,256,128]{2,1,0:T(8,128)(2,1)}, bf16[8,16,256]{2,1,0:T(8,128)(2,1)}) custom-call(bf16[256,1024]{1,0:T(8,128)(2,1)} %refs_0_.3, bf16[16,1024]{1,0:T(8,128)(2,1)} %bitcast.6, bf16[16,1024]{1,0:T(8,128)(2,1)} %bitcast.7, bf16[256,128]{1,0:T(8,128)(2,1)} %refs_3_.1, ...), custom_call_target="tpu_custom_call" | custom-call | tf_op jit(solution)/shard_map/gather/pallas_call | solution.py:436
  20.6 18.8 %attention.1 = (bf16[256,1024]{1,0:T(8,128)(2,1)}, f32[16,256]{1,0:T(8,128)}, bf16[8,16,256]{2,1,0:T(8,128)(2,1)}, f32[16,1024]{1,0:T(8,128)}, f32[16,128]{1,0:T(8,128)}) custom-call(bf16[32,256]{1,0:T(8,128)(2,1)} %get-tuple-element.18.refs_0_, bf16[8,256,128]{2,1,0:T(8,128)(2,1)} %get-tuple-element.19.refs_1_, ...), custom_call_target="tpu_custom_call" | custom-call | tf_op jit(solution)/shard_map/attention/pallas_call | solution.py:461
  39.5 73.8 %reduce.1 = (f32[16,1024]{1,0:T(8,128)}, f32[16,1024]{1,0:T(8,128)}, f32[16,1024]{1,0:T(8,128)}, f32[16,128]{1,0:T(8,128)}) custom-call(bf16[256,1024]{1,0:T(8,128)(2,1)} %refs_0_.3, f32[16,256]{1,0:T(8,128)} %get-tuple-element.23.refs_1_, bf16[8,16,256]{2,1,0:T(8,128)(2,1)} %get-tuple-element.24.refs_2_, f32[16,1024]{1,0:T(8,128)} %get-tuple-element.25.refs_3_, ...), custom_call_target="tpu_custom_call" | custom-call | tf_op jit(solution)/shard_map/reduce/pallas_call | solution.py:487
  113.3 0.0 copy-start.1
  113.3 1.5 %copy.18 = f32[1024,16]{0,1:T(8,128)} copy(f32[1024,16]{0,1:T(8,128)} %bitcast.5) | data formatting | bytes 131072
  114.8 0.0 copy-done.1
  114.8 0.0 copy-start
  114.8 0.6 copy.19
  115.4 0.2 copy-done
  115.7 0.0 copy-start.2
  115.7 0.6 copy.20
  116.3 0.1 copy-done.2
  116.4 0.6 copy.21
Async XLA Ops:
  113.3 1.5 %copy-start.1 = (f32[16,1024]{1,0:T(8,128)S(1)}, f32[16,1024]{1,0:T(8,128)}, u32[]{:S(2)}) copy-start(f32[16,1024]{1,0:T(8,128)} %get-tuple-element.38) | copy-start | bytes 196612
  114.8 0.9 copy-start
  115.7 0.7 copy-start.2

commit v2 on v1

--- a/solution.py
+++ b/solution.py
@@ -148,22 +148,17 @@
     sizes,
     low, keys, frozen_v, lowv, frozen_q, upper_q, upper_v, upstream,
     att, back_q, back_v, grad_uq, grad_uv,
-    q_buf, v_buf, s_buf, p_buf, m_buf, l_buf, o_buf, dq_acc, dq_buf, dv_buf,
+    q_buf, g_buf, v_buf, s_buf, p_buf, m_buf, l_buf, o_buf, dq_buf, gt_buf, dv_buf,
 ):
-    spot = Spot(*sizes)
-    place = spot.place
+    place = Spot(*sizes).place
     rows = frozen_q.shape[0]
     heads = frozen_q.shape[1] // HD
+    rank = upper_q.shape[0]
     scale = float(HD) ** -0.5
-
-    q_buf[...] = (frozen_q[...].astype(F32) + ADAPTER_SCALE * mm(low[0:16, :], upper_q[...], TN)).astype(BF16)
-
-    def value_block(j, carry):
-        v_buf[j] = (frozen_v[j].astype(F32) + ADAPTER_SCALE * mm(lowv[j], upper_v[...], TN)).astype(BF16)
-        dv_buf[j] = jnp.zeros((HD, rows), F32)
-        return carry
-
-    lax.fori_loop(0, place + 1, value_block, 0)
+    gain = scale * 1.4426950408889634
+
+    def part(h):
+        return slice(h * rows, (h + 1) * rows)
 
     def span(j):
         return pl.ds(pl.multiple_of(j * rows, rows), rows)
@@ -177,66 +172,76 @@
             out = f(out, x[:, at : at + HD])
         return out
 
-    def head(h, carry):
-        cols = pl.ds(pl.multiple_of(h * HD, HD), HD)
-        q = q_buf[:, cols]
-        g = upstream[:, cols]
-        s = mm(q, keys[place], NT)
-        causal = lax.broadcasted_iota(jnp.int32, (rows, rows), 0) >= lax.broadcasted_iota(jnp.int32, (rows, rows), 1)
-        s = jnp.where(causal, s, -jnp.inf)
-        s_buf[:, span(place)] = s
-        m_buf[...] = halves(jnp.maximum, s)
-
-        def score(j, carry):
-            s = mm(q, keys[j], NT)
-            s_buf[:, span(j)] = s
-            m_buf[...] = jnp.maximum(m_buf[...], halves(jnp.maximum, s))
-            return carry
-
-        lax.fori_loop(0, place, score, 0)
-        m = jnp.broadcast_to(jnp.max(m_buf[...], axis=1, keepdims=True), (rows, HD))
-        l_buf[...] = jnp.zeros((rows, HD), F32)
-        o_buf[...] = jnp.zeros((rows, HD), F32)
-
-        def weigh(j, carry):
-            p = jnp.exp((s_buf[:, span(j)] - wide(m)) * scale)
-            s_buf[:, span(j)] = p
-            l_buf[...] += halves(jnp.add, p)
+    def row(f, x):
+        return jnp.broadcast_to(f(x, axis=1, keepdims=True), (rows, HD))
+
+    q = (frozen_q[...].astype(F32) + ADAPTER_SCALE * mm(low[0:rank, :], upper_q[...], TN)).astype(BF16)
+    for h in range(heads):
+        q_buf[part(h), :] = q[:, h * HD : (h + 1) * HD]
+
+    def value_block(j, carry):
+        v_buf[j] = (frozen_v[j].astype(F32) + ADAPTER_SCALE * mm(lowv[j], upper_v[...], TN)).astype(BF16)
+        return carry
+
+    lax.fori_loop(0, place + 1, value_block, 0)
+    causal = lax.broadcasted_iota(jnp.int32, (rows, rows), 0) >= lax.broadcasted_iota(jnp.int32, (rows, rows), 1)
+    for h in range(heads):
+        s = jnp.where(causal, mm(q_buf[part(h), :], keys[place], NT), -jnp.inf)
+        s_buf[part(h), span(place)] = s
+        m_buf[part(h), :] = halves(jnp.maximum, s)
+
+    def score(j, carry):
+        for h in range(heads):
+            s = mm(q_buf[part(h), :], keys[j], NT)
+            s_buf[part(h), span(j)] = s
+            m_buf[part(h), :] = jnp.maximum(m_buf[part(h), :], halves(jnp.maximum, s))
+        return carry
+
+    lax.fori_loop(0, place, score, 0)
+    for h in range(heads):
+        m_buf[part(h), :] = row(jnp.max, m_buf[part(h), :])
+        l_buf[part(h), :] = jnp.zeros((rows, HD), F32)
+        o_buf[part(h), :] = jnp.zeros((rows, HD), F32)
+        dq_buf[part(h), :] = jnp.zeros((rows, HD), F32)
+
+    def weigh(j, carry):
+        for h in range(heads):
+            p = jnp.exp2((s_buf[part(h), span(j)] - wide(m_buf[part(h), :])) * gain)
+            s_buf[part(h), span(j)] = p
+            l_buf[part(h), :] += halves(jnp.add, p)
             pb = p.astype(BF16)
-            p_buf[:, span(j)] = pb
-            o_buf[...] += mm(pb, v_buf[j])
-            return carry
-
-        lax.fori_loop(0, place + 1, weigh, 0)
-        inv = jnp.broadcast_to(1.0 / jnp.sum(l_buf[...], axis=1, keepdims=True), (rows, HD))
-        o = (o_buf[...] * inv).astype(BF16)
+            p_buf[part(h), span(j)] = pb
+            o_buf[part(h), :] += mm(pb, v_buf[j])
+        return carry
+
+    lax.fori_loop(0, place + 1, weigh, 0)
+    for h in range(heads):
+        cols = slice(h * HD, (h + 1) * HD)
+        inv = 1.0 / row(jnp.sum, l_buf[part(h), :])
+        o = (o_buf[part(h), :] * inv).astype(BF16)
         att[:, cols] = o
-        gf = g.astype(F32)
-        delta = jnp.broadcast_to(jnp.sum(gf * o.astype(F32), axis=1, keepdims=True), (rows, HD))
-        gt = jnp.transpose((gf * inv).astype(BF16))
-        weight = inv * scale
-        dq_acc[...] = jnp.zeros((rows, HD), F32)
-
-        def back(j, carry):
-            dp = mm(g, v_buf[j], NT)
-            ds = (s_buf[:, span(j)] * ((dp - wide(delta)) * wide(weight))).astype(BF16)
-            dq_acc[...] += mm(ds, keys[j])
-            dv_buf[j] += mm(gt, p_buf[:, span(j)])
-            return carry
-
-        lax.fori_loop(0, place + 1, back, 0)
-        dq_buf[:, cols] = dq_acc[...].astype(BF16)
-        return carry
-
-    lax.fori_loop(0, heads, head, 0)
-    dq = dq_buf[...]
+        g = (upstream[:, cols].astype(F32) * inv).astype(BF16)
+        g_buf[part(h), :] = g
+        gt_buf[:, part(h)] = jnp.transpose(g)
+        m_buf[part(h), :] = row(jnp.sum, g.astype(F32) * o.astype(F32))
+
+    def back(j, carry):
+        for h in range(heads):
+            dp = mm(g_buf[part(h), :], v_buf[j], NT)
+            ds = (s_buf[part(h), span(j)] * (dp - wide(m_buf[part(h), :]))).astype(BF16)
+            dq_buf[part(h), :] += mm(ds, keys[j])
+        dv_buf[j] = mm(gt_buf[...], p_buf[:, span(j)]).astype(BF16)
+        return carry
+
+    lax.fori_loop(0, place + 1, back, 0)
+    dq = jnp.concatenate([(dq_buf[part(h), :] * scale).astype(BF16) for h in range(heads)], axis=1)
     back_q[...] = mm(upper_q[...], dq, NT)
-    grad_uq[...] = mm(low[0:16, :], dq) * ADAPTER_SCALE
+    grad_uq[...] = mm(low[0:rank, :], dq) * ADAPTER_SCALE
     grad_uv[...] = jnp.zeros_like(grad_uv)
     back_v[...] = jnp.zeros_like(back_v)
 
     def value_back(j, carry):
-        dv = dv_buf[j].astype(BF16)
+        dv = dv_buf[j]
         back_v[j] = mm(upper_v[...], dv).astype(BF16)
         grad_uv[...] += mm(lowv[j], dv, NT) * ADAPTER_SCALE
         return carry
@@ -422,6 +427,7 @@
 ):
     rows, width = hidden_in.shape
     rank = down_query.shape[1]
+    heads = frozen_query.shape[1] // HD
     seq_count, count = lax.axis_size("seq"), lax.axis_size("tensor")
     members = GROUP // rows
     sizes = (seq_count, count, members)
@@ -470,16 +476,17 @@
         in_specs=[vmem] * 8,
         out_specs=(vmem,) * 5,
         scratch_shapes=[
-            pltpu.VMEM((rows, width), BF16),
+            pltpu.VMEM((heads * rows, HD), BF16),
+            pltpu.VMEM((heads * rows, HD), BF16),
             pltpu.VMEM((members, rows, HD), BF16),
-            pltpu.VMEM((rows, GROUP), F32),
-            pltpu.VMEM((rows, GROUP), BF16),
-            pltpu.VMEM((rows, HD), F32),
-            pltpu.VMEM((rows, HD), F32),
-            pltpu.VMEM((rows, HD), F32),
-            pltpu.VMEM((rows, HD), F32),
-            pltpu.VMEM((rows, width), BF16),
-            pltpu.VMEM((members, HD, rows), F32),
+            pltpu.VMEM((heads * rows, GROUP), F32),
+            pltpu.VMEM((heads * rows, GROUP), BF16),
+            pltpu.VMEM((heads * rows, HD), F32),
+            pltpu.VMEM((heads * rows, HD), F32),
+            pltpu.VMEM((heads * rows, HD), F32),
+            pltpu.VMEM((heads * rows, HD), F32),
+            pltpu.VMEM((HD, heads * rows), BF16),
+            pltpu.VMEM((members, HD, rows), BF16),
         ],
         name="attention",
     )(low, keys, frozen_v, lowv, frozen_query, query_upper_factor, value_upper_factor, grad_output)

time: 117 us -> 83.9 us (0.72)
  Pallas kernels: 113 us -> 79.2 us
    pallas_call x1, Pallas kernels: 73.8 us -> 49.6 us  [per_device(): pl.pallas_call(lambda *refs: reduce_kernel(sizes, *refs), out_shape=(shap...]
    pallas_call x1, Pallas kernels: 18.8 us -> 9.62 us  [per_device(): pl.pallas_call(lambda *refs: attention_kernel(sizes, *refs), out_shape=(s...]
where the time goes in v2:
time: 83.9 us; the launch traced here: 83.6 us
  Pallas kernels  79.2 us (94%)
  local copies, waits for them, and re-layouts  3.67 us (4%)
    pallas_call x1, Pallas kernels, per_device(): pl.pallas_call(lambda *refs: reduce_kernel(sizes, *refs), out_shape=(shap...  49.6 us
    pallas_call x1, Pallas kernels, per_device(): pl.pallas_call(lambda *refs: gather_kernel(sizes, *refs), out_shape=(shap...  20 us
    pallas_call x1, Pallas kernels, per_device(): pl.pallas_call(lambda *refs: attention_kernel(sizes, *refs), out_shape=(s...  9.62 us
    unnamed x10, local copies, waits for them, and re-layouts  3.67 us

profile of v2, /device:TPU:1, one launch (start us, length us, event | category | flops | bytes accessed | tf_op | source)
XLA Modules:
  0.0 83.6 jit_solution(5071578853092727569)
XLA Ops:
  0.6 20.0 %gather.1 = (bf16[32,256]{1,0:T(8,128)(2,1)}, bf16[8,256,128]{2,1,0:T(8,128)(2,1)}, bf16[8,256,128]{2,1,0:T(8,128)(2,1)}, bf16[8,16,256]{2,1,0:T(8,128)(2,1)}) custom-call(bf16[256,1024]{1,0:T(8,128)(2,1)} %refs_0_.3, bf16[16,1024]{1,0:T(8,128)(2,1)} %bitcast.6, bf16[16,1024]{1,0:T(8,128)(2,1)} %bitcast.7, bf16[256,128]{1,0:T(8,128)(2,1)} %refs_3_.1, ...), custom_call_target="tpu_custom_call" | custom-call | tf_op jit(solution)/shard_map/gather/pallas_call | solution.py:442
  20.6 9.6 %attention.1 = (bf16[256,1024]{1,0:T(8,128)(2,1)}, f32[16,256]{1,0:T(8,128)}, bf16[8,16,256]{2,1,0:T(8,128)(2,1)}, f32[16,1024]{1,0:T(8,128)}, f32[16,128]{1,0:T(8,128)}) custom-call(bf16[32,256]{1,0:T(8,128)(2,1)} %get-tuple-element.18.refs_0_, bf16[8,256,128]{2,1,0:T(8,128)(2,1)} %get-tuple-element.19.refs_1_, ...), custom_call_target="tpu_custom_call" | custom-call | tf_op jit(solution)/shard_map/attention/pallas_call | solution.py:467
  30.2 49.6 %reduce.1 = (f32[16,1024]{1,0:T(8,128)}, f32[16,1024]{1,0:T(8,128)}, f32[16,1024]{1,0:T(8,128)}, f32[16,128]{1,0:T(8,128)}) custom-call(bf16[256,1024]{1,0:T(8,128)(2,1)} %refs_0_.3, f32[16,256]{1,0:T(8,128)} %get-tuple-element.23.refs_1_, bf16[8,16,256]{2,1,0:T(8,128)(2,1)} %get-tuple-element.24.refs_2_, f32[16,1024]{1,0:T(8,128)} %get-tuple-element.25.refs_3_, ...), custom_call_target="tpu_custom_call" | custom-call | tf_op jit(solution)/shard_map/reduce/pallas_call | solution.py:494
  79.9 0.0 copy-start.1
  79.9 1.5 %copy.18 = f32[1024,16]{0,1:T(8,128)} copy(f32[1024,16]{0,1:T(8,128)} %bitcast.5) | data formatting | bytes 131072
  81.4 0.0 copy-done.1
  81.4 0.0 copy-start
  81.4 0.6 copy.19
  82.0 0.2 copy-done
  82.3 0.0 copy-start.2
  82.3 0.6 copy.20
  82.9 0.1 copy-done.2
  83.0 0.6 copy.21
Async XLA Ops:
  79.9 1.5 %copy-start.1 = (f32[16,1024]{1,0:T(8,128)S(1)}, f32[16,1024]{1,0:T(8,128)}, u32[]{:S(2)}) copy-start(f32[16,1024]{1,0:T(8,128)} %get-tuple-element.38) | copy-start | bytes 196612
  81.4 0.9 %copy-start = (f32[16,1024]{1,0:T(8,128)S(1)}, f32[16,1024]{1,0:T(8,128)}, u32[]{:S(2)}) copy-start(f32[16,1024]{1,0:T(8,128)} %get-tuple-element.29) | copy-start | bytes 196612
  82.3 0.7 copy-start.2
